TPU v7x, 32 devices: a whole 2x2x4 slice. The times are simulated.
32 devices in a mesh: sector: 8 (over y, x, core), term: 4 (over z).
Axes of the slice: x: 2, y: 2, z: 4, core: 2. Of those that a mesh axis runs over, the one named last changes fastest.
Arguments:
- blocks: bfloat16 [5120, 640], P('sector'), may hold values from -6 to 6
- left_env: bfloat16 [8, 4, 640, 1920], P('sector', 'term'), may hold values from -0.125 to 0.125
- right_env: bfloat16 [8, 4, 640, 640], P('sector', 'term'), may hold values from -0.125 to 0.125
- coupling: int32 [8, 3], P('sector'), may hold values 0 or 1
- widths: int32 [8], P('sector'), may hold values from 320 to 640
Outputs:
- filtered: bfloat16 [5120, 640], P('sector')
All inputs are finite; a program needn't handle non-finite values. No bound on the sum of `coupling` on one device may be relied on, other than what follows from the above.
Results may differ from a plain program's by a relative error of at most 0.005.
Values may be sent and summed in bfloat16 or wider, within the bound.
A program may use at most 64 MiB of HBM per device.

v0:
```python
import jax
import jax.numpy as jnp
from jax import lax
from jax.sharding import PartitionSpec as P


def with_halo(x, sides, width):
    for axis, dim in sides:
        count, length = (lax.axis_size(axis), x.shape[dim])
        up = [(i, (i + 1) % count) for i in range(count - 1)]
        down = [(j, i) for i, j in up]
        last = lax.slice_in_dim(x, length - width, length, axis=dim)
        leading = lax.slice_in_dim(x, 0, width, axis=dim)
        before = lax.ppermute(last, axis, up)
        after = lax.ppermute(leading, axis, down)
        x = jnp.concatenate([before, x, after], axis=dim)
    return x


def keep_live(values, live_width):
    row_index = lax.broadcasted_iota(jnp.int32, values.shape, 0)
    col_index = lax.broadcasted_iota(jnp.int32, values.shape, 1)
    return jnp.where(
        (row_index < live_width) & (col_index < live_width), values, jnp.zeros_like(values)
    )


def contract(stacked, left_part, right_part):
    partial_value = jnp.einsum(
        "tik,kj->tij", left_part, stacked, preferred_element_type=jnp.float32
    ).astype(jnp.bfloat16)
    return jnp.einsum("tij,tjl->il", partial_value, right_part, preferred_element_type=jnp.float32)


def shards(blocks, left_env, right_env, coupling, widths):
    block_side = blocks.shape[1]
    left_part = left_env[0]
    right_part = right_env[0]
    live_width = widths[0]
    row_scale = jnp.repeat(coupling[0].astype(jnp.bfloat16), block_side)

    def full_apply(source):
        nearby = with_halo(source, (("sector", 0),), source.shape[0])
        term_sum = lax.psum(contract(nearby * row_scale[:, None], left_part, right_part), "term")
        return keep_live(term_sum, live_width)

    first_pass = full_apply(blocks).astype(jnp.bfloat16)
    return (2.0 * full_apply(first_pass) - blocks.astype(jnp.float32)).astype(jnp.bfloat16)


def solution(mesh):
    placed = (
        P("sector", None),
        P("sector", "term", None, None),
        P("sector", "term", None, None),
        P("sector", None),
        P("sector"),
    )
    return jax.shard_map(
        shards, mesh=mesh, in_specs=placed, out_specs=P("sector", None), check_vma=False
    )
```

profile of v0, /device:TPU:4, one launch (start us, length us, event | category | flops | bytes accessed | tf_op | source)
XLA Modules:
  0.0 207.5 jit_solution(17464523039539221608)
XLA Ops:
  6.5 0.0 copy-start
  6.5 0.0 all-reduce.3.cloned.1.call-start
  6.5 2.9 %collective-permute-start.1 = (bf16[640,640]{1,0:T(8,128)(2,1)}, bf16[640,640]{1,0:T(8,128)(2,1)}, u32[]{:S(2)}, u32[]{:S(2)}) collective-permute-start(bf16[640,640]{1,0:T(8,128)(2,1)} %param.5), channel_id=1, source_target_pairs={{4,0},{8,4},{12,8},{16,12},{20,16},{24,20},{28,24},{5,1},{9,5},{13... | collective-permute-start | bytes 2457608 | tf_op jit(solution)/shard_map/ppermute | solution.py:15
  9.5 1.9 collective-permute-start
  12.0 0.7 convert_bitcast_fusion
  12.7 0.1 broadcast_in_dim.3
  12.8 13.6 %collective-permute-done.1 = bf16[640,640]{1,0:T(8,128)(2,1)} collective-permute-done((bf16[640,640]{1,0:T(8,128)(2,1)}, bf16[640,640]{1,0:T(8,128)(2,1)}, u32[]{:S(2)}, u32[]{:S(2)}) %collective-permute-start.1) | collective-permute-done | bytes 819232 | tf_op jit(solution)/shard_map/ppermute | solution.py:15
  26.4 3.0 %collective-permute-done = bf16[640,640]{1,0:T(8,128)(2,1)} collective-permute-done((bf16[640,640]{1,0:T(8,128)(2,1)}, bf16[640,640]{1,0:T(8,128)(2,1)}, u32[]{:S(2)}, u32[]{:S(2)}) %collective-permute-start) | collective-permute-done | bytes 819232 | tf_op jit(solution)/shard_map/ppermute | solution.py:14
  29.4 0.0 copy-done
  29.4 7.2 %fusion.23 = f32[640,640]{1,0:T(8,128)} fusion(bf16[1,1,640,1920]{3,2,1,0:T(8,128)(2,1)S(1)} %copy-done, bf16[640,640]{1,0:T(8,128)(2,1)} %collective-permute-done.1, bf16[640,640]{1,0:T(8,128)(2,1)} %param.5, bf16[640,640]{1,0:T(8,128)(2,1)} %collective-permute-done, bf16[1920]{0:T(1024)(128)(2,1)S(1)} %mul.22, bf16[1,1,640,640]{3,2,1,0:T(8,128)(2,1)} %param.7), kind=kOutput, calls=%fused_computation.22 | convolution fusion | flops 2107392000 | bytes 7376640 | tf_op jit(solution)/shard_map/tij,tjl->il/dot_general | solution.py:32
  36.7 62.0 %all-reduce.4 = bf16[640,640]{1,0:T(8,128)(2,1)S(1)} all-reduce(f32[640,640]{1,0:T(8,128)} %fusion.23), channel_id=1, replica_groups=mesh['sector'=8,'term'=4] {'term'}, use_global_device_ids=true, to_apply=%region_0.0 | all-reduce | flops 409600 | bytes 2457600 | tf_op jit(solution)/shard_map/psum | solution.py:44
  98.6 0.3 fusion.12
  98.9 0.0 copy-start.2
  99.0 0.0 copy-start.1
  99.0 2.1 collective-permute-start.3
  101.0 0.0 copy-done.2
  101.0 2.4 %collective-permute-start.2 = (bf16[640,640]{1,0:T(8,128)(2,1)S(1)}, bf16[640,640]{1,0:T(8,128)(2,1)}, u32[]{:S(2)}, u32[]{:S(2)}) collective-permute-start(bf16[640,640]{1,0:T(8,128)(2,1)S(1)} %fusion.12), channel_id=1, source_target_pairs={{0,4},{4,8},{8,12},{12,16},{16,20},{20,24},{24,28},{1,5},{5,9},{9,... | collective-permute-start | bytes 2457608 | tf_op jit(solution)/shard_map/ppermute | solution.py:14
  103.5 14.4 %collective-permute-done.3 = bf16[640,640]{1,0:T(8,128)(2,1)S(1)} collective-permute-done((bf16[640,640]{1,0:T(8,128)(2,1)S(1)}, bf16[640,640]{1,0:T(8,128)(2,1)S(1)}, u32[]{:S(2)}, u32[]{:S(2)}) %collective-permute-start.3) | collective-permute-done | bytes 819232 | tf_op jit(solution)/shard_map/ppermute | solution.py:15
  117.9 0.9 copy-done.3
  118.8 0.0 collective-permute-done.2
  118.8 7.2 %fusion.26 = f32[640,640]{1,0:T(8,128)} fusion(bf16[1,1,640,1920]{3,2,1,0:T(8,128)(2,1)S(1)} %copy-done, bf16[640,640]{1,0:T(8,128)(2,1)} %copy-done.3, bf16[640,640]{1,0:T(8,128)(2,1)} %copy-done.2, bf16[640,640]{1,0:T(8,128)(2,1)} %collective-permute-done.2, bf16[1920]{0:T(1024)(128)(2,1)S(1)} %mul.22, bf16[1,1,640,640]{3,2,1,0:T(8,128)(2,1)} %param.7), kind=kOutput, calls=%fused_computation.23 | convolution fusion | flops 2107392000 | bytes 7376640 | tf_op jit(solution)/shard_map/tij,tjl->il/dot_general | solution.py:32
  126.0 0.0 all-reduce.3.cloned.1.call-update
  126.1 71.9 %all-reduce.3.cloned.1.call-done = f32[640,640]{1,0:T(8,128)} async-done(((f32[640,640]{1,0:T(8,128)}), f32[640,640]{1,0:T(8,128)}) %all-reduce.3.cloned.1.call-update) | async-done | bytes 1638416 | tf_op jit(solution)/shard_map/psum | solution.py:44
  197.9 2.7 %fusion.15 = bf16[640,640]{1,0:T(8,128)(2,1)} fusion(f32[640,640]{1,0:T(8,128)} %all-reduce.3.cloned.1.call-done, bf16[640,640]{1,0:T(8,128)(2,1)S(1)} %copy-done.1, pred[640]{0:T(1024)(128)(4,1)S(1)} %iota_compare_fusion), kind=kLoop, calls=%fused_computation.19 | loop fusion | flops 2457600 | bytes 3277440 | tf_op jit(solution)/shard_map/convert_element_type | solution.py:48
  (4 shorter events, 0.0 us)
Async XLA Ops:
  6.5 22.9 %copy-start = (bf16[1,1,640,1920]{3,2,1,0:T(8,128)(2,1)S(1)}, bf16[1,1,640,1920]{3,2,1,0:T(8,128)(2,1)}, u32[]{:S(2)}) copy-start(bf16[1,1,640,1920]{3,2,1,0:T(8,128)(2,1)} %param.6) | copy-start | bytes 7372804
  6.5 191.4 %all-reduce.3.cloned.1.call-start = ((), (), s32[]{:S(2)}) async-start(), calls=%async_computation | async-start | bytes 3276800 | tf_op jit(solution)/shard_map/psum | solution.py:44
  6.5 19.9 %collective-permute-start.1 = (bf16[640,640]{1,0:T(8,128)(2,1)}, bf16[640,640]{1,0:T(8,128)(2,1)}, u32[]{:S(2)}, u32[]{:S(2)}) collective-permute-start(bf16[640,640]{1,0:T(8,128)(2,1)} %param.5), channel_id=1, source_target_pairs={{4,0},{8,4},{12,8},{16,12},{20,16},{24,20},{28,24},{5,1},{9,5},{13... | collective-permute-start | bytes 2457608 | tf_op jit(solution)/shard_map/ppermute | solution.py:15
  9.5 20.0 %collective-permute-start = (bf16[640,640]{1,0:T(8,128)(2,1)}, bf16[640,640]{1,0:T(8,128)(2,1)}, u32[]{:S(2)}, u32[]{:S(2)}) collective-permute-start(bf16[640,640]{1,0:T(8,128)(2,1)} %param.5), channel_id=1, source_target_pairs={{0,4},{4,8},{8,12},{12,16},{16,20},{20,24},{24,28},{1,5},{5,9},{9,... | collective-permute-start | bytes 2457608 | tf_op jit(solution)/shard_map/ppermute | solution.py:14
  98.9 2.1 %copy-start.2 = (bf16[640,640]{1,0:T(8,128)(2,1)}, bf16[640,640]{1,0:T(8,128)(2,1)S(1)}, u32[]{:S(2)}) copy-start(bf16[640,640]{1,0:T(8,128)(2,1)S(1)} %fusion.12) | copy-start | bytes 2457604
  99.0 99.0 %copy-start.1 = (bf16[640,640]{1,0:T(8,128)(2,1)S(1)}, bf16[640,640]{1,0:T(8,128)(2,1)}, u32[]{:S(2)}) copy-start(bf16[640,640]{1,0:T(8,128)(2,1)} %param.5) | copy-start | bytes 2457604
  99.0 18.9 %collective-permute-start.3 = (bf16[640,640]{1,0:T(8,128)(2,1)S(1)}, bf16[640,640]{1,0:T(8,128)(2,1)S(1)}, u32[]{:S(2)}, u32[]{:S(2)}) collective-permute-start(bf16[640,640]{1,0:T(8,128)(2,1)S(1)} %fusion.12), channel_id=1, source_target_pairs={{4,0},{8,4},{12,8},{16,12},{20,16},{24,20},{28,24},{5,1},{9,5},{13... | collective-permute-start | bytes 2457608 | tf_op jit(solution)/shard_map/ppermute | solution.py:15
  101.0 17.7 %collective-permute-start.2 = (bf16[640,640]{1,0:T(8,128)(2,1)S(1)}, bf16[640,640]{1,0:T(8,128)(2,1)}, u32[]{:S(2)}, u32[]{:S(2)}) collective-permute-start(bf16[640,640]{1,0:T(8,128)(2,1)S(1)} %fusion.12), channel_id=1, source_target_pairs={{0,4},{4,8},{8,12},{12,16},{16,20},{20,24},{24,28},{1,5},{5,9},{9,... | collective-permute-start | bytes 2457608 | tf_op jit(solution)/shard_map/ppermute | solution.py:14
  117.9 0.9 copy-start.3
Sparse Core Ops, SparseCore 0:
  126.2 71.6 all-reduce.2
where the time goes:
time: 209 us; the launch traced here: 208 us
  waiting for transfers between devices  103 us (49%)
  blocking collectives  62 us (30%)
  matrix products  14.5 us (7%)
  between operations  14.1 us (7%)
  starting transfers between devices  9.29 us (4%)
  other arithmetic  3.72 us (2%)
    psum x1, waiting for transfers between devices, full_apply(): lax.psum(contract(nearby * row_scale[:, None], left_part, right_part), 't...  71.9 us
    psum x1, blocking collectives, full_apply(): lax.psum(contract(nearby * row_scale[:, None], left_part, right_part), 't...  62 us
    ppermute x2, waiting for transfers between devices, with_halo(): after = lax.ppermute(leading, axis, down)  28.1 us
    dot_general x2, matrix products, contract(): jnp.einsum('tij,tjl->il', partial_value, right_part, preferred_element_ty...  14.5 us
    ppermute x2, starting transfers between devices, with_halo(): after = lax.ppermute(leading, axis, down)  4.96 us
    ppermute x2, starting transfers between devices, with_halo(): before = lax.ppermute(last, axis, up)  4.33 us
  transfers between devices with their start and end apart: 5, of which 4 were waited for; matrix products, arithmetic and copies ran while one was open for 0% of the time, Pallas kernels for 0%

commit v1 on v0

v1 whole, which is shorter than its diff:
```python
import functools

import jax
import jax.numpy as jnp
from jax import lax
from jax.experimental import pallas as pl
from jax.experimental.pallas import tpu as pltpu
from jax.sharding import PartitionSpec as P

MESH = pl.DeviceIdType.MESH
PIECE = 32


def kernel(n_s, n_t, pieces, blocks_ref, left_ref, right_ref, coup_ref, width_ref, out_ref,
           lbuf, rbuf, st1, st2, sbuf, recv, send, obuf,
           lsem, osem, h1s, h1r, rss, rsr, ags, agr, h2s, h2r):
    s = lax.axis_index("sector")
    z = lax.axis_index("term")
    side = blocks_ref.shape[0]
    half = side // 2
    pr = half // pieces
    has_lo, has_hi = s > 0, s < n_s - 1
    has_dn, has_up = z > 0, z < n_t - 1

    def to_sector(d):
        return (s + d, z)

    own1 = st1.at[pl.ds(side, side), :]
    cp_own = pltpu.make_async_copy(blocks_ref, own1, lsem.at[0])
    cp_l = pltpu.make_async_copy(left_ref.at[0, 0], lbuf, lsem.at[1])
    cp_r = pltpu.make_async_copy(right_ref.at[0, 0], rbuf, lsem.at[2])
    cp_own.start()
    cp_l.start()
    cp_r.start()

    barrier = pltpu.get_barrier_semaphore()
    for cond, dev in ((has_lo, (s - 1, z)), (has_hi, (s + 1, z)), (has_dn, (s, z - 1)), (has_up, (s, z + 1))):
        @pl.when(cond)
        def _():
            pl.semaphore_signal(barrier, inc=1, device_id=dev, device_id_type=MESH)
    count = (has_lo.astype(jnp.int32) + has_hi.astype(jnp.int32)
             + has_dn.astype(jnp.int32) + has_up.astype(jnp.int32))
    pl.semaphore_wait(barrier, count)

    def halo1(d):
        group = 2 if d < 0 else 0
        slot = 0 if d < 0 else 1
        return pltpu.make_async_remote_copy(
            src_ref=blocks_ref, dst_ref=st1.at[pl.ds(group * side, side), :],
            send_sem=h1s.at[slot], recv_sem=h1r.at[slot],
            device_id=to_sector(d), device_id_type=MESH)

    @pl.when(has_lo)
    def _():
        halo1(-1).start()

    @pl.when(has_hi)
    def _():
        halo1(1).start()

    zeros = jnp.zeros((side, side), st1.dtype)

    @pl.when(jnp.logical_not(has_lo))
    def _():
        st1[pl.ds(0, side), :] = zeros
        st2[pl.ds(0, side), :] = zeros

    @pl.when(jnp.logical_not(has_hi))
    def _():
        st1[pl.ds(2 * side, side), :] = zeros
        st2[pl.ds(2 * side, side), :] = zeros

    width = width_ref[0]
    cp_l.wait()
    for k in range(3):
        c = coup_ref[0, k].astype(jnp.float32)
        cols = pl.ds(k * side, side)
        lbuf[:, cols] = (lbuf[:, cols].astype(jnp.float32) * c).astype(lbuf.dtype)
    cp_own.wait()
    cp_r.wait()

    x = jnp.where(z * 2 < n_t, 1, 0)
    flows = (x, 1 - x)

    def has_prev(f):
        return jnp.where(f == 1, z, n_t - 1 - z) > 0

    def has_next(f):
        return jnp.where(f == 1, n_t - 1 - z, z) > 0

    def rows_of(f, i):
        return pl.ds(pl.multiple_of(f * half + i * pr, pr), pr)

    def contract(st, f):
        base = pl.ds(pl.multiple_of(f * half, half), half)
        t = jnp.dot(lbuf[base, :], st[...], preferred_element_type=jnp.float32).astype(jnp.bfloat16)
        sbuf[base, :] = jnp.dot(t, rbuf[...], preferred_element_type=jnp.float32)

    def rs_copy(a, f, i):
        r = rows_of(f, i)
        return pltpu.make_async_remote_copy(
            src_ref=send.at[a, r, :], dst_ref=recv.at[a, r, :],
            send_sem=rss.at[a, f, i], recv_sem=rsr.at[a, f, i],
            device_id=(s, z + 2 * f - 1), device_id_type=MESH)

    def result(a, f, i):
        if a == 0:
            return st2.at[pl.ds(pl.multiple_of(side + f * half + i * pr, pr), pr), :]
        return obuf.at[rows_of(f, i), :]

    def ag_copy(a, f, i):
        return pltpu.make_async_remote_copy(
            src_ref=result(a, f, i), dst_ref=result(a, f, i),
            send_sem=ags.at[a, f, i], recv_sem=agr.at[a, f, i],
            device_id=(s, z - 2 * f + 1), device_id_type=MESH)

    def halo2(d, f, i):
        group = 2 if d < 0 else 0
        slot = 0 if d < 0 else 1
        dst = pl.ds(pl.multiple_of(group * side + f * half + i * pr, pr), pr)
        return pltpu.make_async_remote_copy(
            src_ref=result(0, f, i), dst_ref=st2.at[dst, :],
            send_sem=h2s.at[slot, f, i], recv_sem=h2r.at[slot, f, i],
            device_id=to_sector(d), device_id_type=MESH)

    def out_copy(f, i):
        return pltpu.make_async_copy(obuf.at[rows_of(f, i), :], out_ref.at[rows_of(f, i), :], osem.at[f, i])

    def publish(a, f, i):
        if a == 0:
            @pl.when(has_lo)
            def _():
                halo2(-1, f, i).start()

            @pl.when(has_hi)
            def _():
                halo2(1, f, i).start()
        else:
            out_copy(f, i).start()

    def reduce_step(a, f, i):
        r = rows_of(f, i)

        @pl.when(has_prev(f))
        def _():
            rs_copy(a, f, i).wait_recv()
            sbuf[r, :] = sbuf[r, :] + recv[a, r, :].astype(jnp.float32)

        @pl.when(has_next(f))
        def _():
            send[a, r, :] = sbuf[r, :].astype(send.dtype)
            rs_copy(a, f, i).start()

        @pl.when(jnp.logical_not(has_next(f)))
        def _():
            value = sbuf[r, :]
            row = f * half + i * pr + lax.broadcasted_iota(jnp.int32, value.shape, 0)
            col = lax.broadcasted_iota(jnp.int32, value.shape, 1)
            value = jnp.where((row < width) & (col < width), value, jnp.zeros_like(value))
            if a == 1:
                start = st1[pl.ds(pl.multiple_of(side + f * half + i * pr, pr), pr), :]
                value = 2.0 * value - start.astype(jnp.float32)
            result(a, f, i)[...] = value.astype(st2.dtype)

            @pl.when(has_prev(f))
            def _():
                ag_copy(a, f, i).start()
            publish(a, f, i)

    def gather_step(a, f, i):
        @pl.when(has_next(f))
        def _():
            ag_copy(a, f, i).wait_recv()

            @pl.when(has_prev(f))
            def _():
                ag_copy(a, f, i).start()
            publish(a, f, i)

    def loop(body):
        def step(i, c):
            body(i)
            return c
        lax.fori_loop(0, pieces, step, 0)

    def apply(a, st):
        fx, fy = flows
        contract(st, fx)

        @pl.when(jnp.logical_not(has_prev(fx)))
        def _():
            loop(lambda i: reduce_step(a, fx, i))

        contract(st, fy)

        def both(i):
            @pl.when(has_prev(fx))
            def _():
                reduce_step(a, fx, i)
            reduce_step(a, fy, i)
        loop(both)

        def gather(i):
            gather_step(a, fy, i)
            gather_step(a, fx, i)
        loop(gather)

    @pl.when(has_lo)
    def _():
        halo1(1).wait_recv()

    @pl.when(has_hi)
    def _():
        halo1(-1).wait_recv()
    apply(0, st1)

    def arrived(i):
        for f in flows:
            @pl.when(has_lo)
            def _():
                halo2(1, f, i).wait_recv()

            @pl.when(has_hi)
            def _():
                halo2(-1, f, i).wait_recv()
    loop(arrived)
    apply(1, st2)

    def drain(i):
        for f in (0, 1):
            for a in (0, 1):
                @pl.when(has_next(f))
                def _():
                    rs_copy(a, f, i).wait_send()

                @pl.when(has_prev(f))
                def _():
                    ag_copy(a, f, i).wait_send()

            @pl.when(has_lo)
            def _():
                halo2(-1, f, i).wait_send()

            @pl.when(has_hi)
            def _():
                halo2(1, f, i).wait_send()
            out_copy(f, i).wait()
    loop(drain)

    @pl.when(has_lo)
    def _():
        halo1(-1).wait_send()

    @pl.when(has_hi)
    def _():
        halo1(1).wait_send()


def shards(n_s, n_t, blocks, left_env, right_env, coupling, widths):
    side = blocks.shape[1]
    pieces = side // 2 // PIECE
    dma = pltpu.SemaphoreType.DMA
    any_space = pl.BlockSpec(memory_space=pl.ANY)
    smem = pl.BlockSpec(memory_space=pltpu.SMEM)
    return pl.pallas_call(
        functools.partial(kernel, n_s, n_t, pieces),
        out_shape=jax.ShapeDtypeStruct(blocks.shape, blocks.dtype),
        in_specs=[any_space, any_space, any_space, smem, smem],
        out_specs=any_space,
        scratch_shapes=[
            pltpu.VMEM((side, 3 * side), jnp.bfloat16),
            pltpu.VMEM((side, side), jnp.bfloat16),
            pltpu.VMEM((3 * side, side), jnp.bfloat16),
            pltpu.VMEM((3 * side, side), jnp.bfloat16),
            pltpu.VMEM((side, side), jnp.float32),
            pltpu.VMEM((2, side, side), jnp.bfloat16),
            pltpu.VMEM((2, side, side), jnp.bfloat16),
            pltpu.VMEM((side, side), jnp.bfloat16),
            dma((3,)), dma((2, pieces)), dma((2,)), dma((2,)),
            dma((2, 2, pieces)), dma((2, 2, pieces)),
            dma((2, 2, pieces)), dma((2, 2, pieces)),
            dma((2, 2, pieces)), dma((2, 2, pieces)),
        ],
        compiler_params=pltpu.CompilerParams(collective_id=0, has_side_effects=True),
    )(blocks, left_env, right_env, coupling, widths)


def solution(mesh):
    placed = (
        P("sector", None),
        P("sector", "term", None, None),
        P("sector", "term", None, None),
        P("sector", None),
        P("sector"),
    )
    body = functools.partial(shards, mesh.shape["sector"], mesh.shape["term"])
    return jax.shard_map(body, mesh=mesh, in_specs=placed, out_specs=P("sector", None), check_vma=False)
```

time: 209 us -> 168 us (0.80)
  Pallas kernels: 0 us -> 164 us
  waiting for transfers between devices: 103 us -> 0 us
  blocking collectives: 62 us -> 0 us
  matrix products: 14.5 us -> 0 us
  between operations: 14.1 us -> 0.66 us
  starting transfers between devices: 9.29 us -> 0 us
  other arithmetic: 3.72 us -> 0 us
    pallas_call x0 -> x1, Pallas kernels: none -> 164 us  [shards(): pl.pallas_call(functools.partial(kernel, n_s, n_t, pieces), out_shape=jax...]
    psum x1 -> x0, waiting for transfers between devices: 71.9 us -> none  [full_apply(): lax.psum(contract(nearby * row_scale[:, None], left_part, right_part), 't...]
    psum x1 -> x0, blocking collectives: 62 us -> none  [full_apply(): lax.psum(contract(nearby * row_scale[:, None], left_part, right_part), 't...]
    ppermute x4 -> x0, waiting for transfers between devices: 31.1 us -> none  [the longest x2 28.1 us: with_halo(): after = lax.ppermute(leading, axis, down)]
    dot_general x2 -> x0, matrix products: 14.5 us -> none  [contract(): jnp.einsum('tij,tjl->il', partial_value, right_part, preferred_element_ty...]
    ppermute x4 -> x0, starting transfers between devices: 9.29 us -> none  [the longest x2 4.96 us: with_halo(): after = lax.ppermute(leading, axis, down)]
    convert_element_type x3 -> x0, other arithmetic: 3.72 us -> none  [the longest x1 2.74 us: shards(): (2.0 * full_apply(first_pass) - blocks.astype(jnp.float32)).astype(jnp.bf...]
  transfers between devices with their start and end apart: 5 -> 0, of which waited for: 4 -> 0; matrix products, arithmetic and copies ran while one was open for 0% -> 0% of each run, Pallas kernels for 0% -> 0%
where the time goes in v1:
time: 168 us; the launch traced here: 167 us
  Pallas kernels  164 us (98%)
  local copies, waits for them, and re-layouts  2.11 us (1%)
    pallas_call x1, Pallas kernels, shards(): pl.pallas_call(functools.partial(kernel, n_s, n_t, pieces), out_shape=jax...  164 us

profile of v1, /device:TPU:4, one launch (start us, length us, event | category | flops | bytes accessed | tf_op | source)
XLA Modules:
  0.0 166.9 jit_solution(7666831935778937311)
XLA Ops:
  0.7 164.1 %shard_map.55 = bf16[640,640]{1,0:T(8,128)(2,1)} custom-call(bf16[640,640]{1,0:T(8,128)(2,1)} %blocks_ref.1, bf16[1,1,640,1920]{3,2,1,0:T(8,128)(2,1)} %left_ref.1, bf16[1,1,640,640]{3,2,1,0:T(8,128)(2,1)} %right_ref.1, s32[1,3]{1,0:T(1,128)} %coup_ref.1, s32[1]{0:T(128)S(6)} %copy.7.width_ref), custom_call_target="tpu_custom_call" | custom-call | tf_op jit(solution)/shard_map/pallas_call | solution.py:265
  164.8 2.1 %copy.8 = bf16[640,640]{1,0:T(8,128)(2,1)} copy(bf16[640,640]{1,0:T(8,128)(2,1)} %shard_map.55) | data formatting | bytes 1638400

commit v2 on v1

--- a/solution.py
+++ b/solution.py
@@ -9,6 +9,7 @@
 
 MESH = pl.DeviceIdType.MESH
 PIECE = 32
+LAG = 4
 
 
 def kernel(n_s, n_t, pieces, blocks_ref, left_ref, right_ref, coup_ref, width_ref, out_ref,
@@ -82,8 +83,11 @@
     x = jnp.where(z * 2 < n_t, 1, 0)
     flows = (x, 1 - x)
 
+    def far(f):
+        return jnp.where(f == 1, z, n_t - 1 - z)
+
     def has_prev(f):
-        return jnp.where(f == 1, z, n_t - 1 - z) > 0
+        return far(f) > 0
 
     def has_next(f):
         return jnp.where(f == 1, n_t - 1 - z, z) > 0
@@ -193,17 +197,22 @@
 
         contract(st, fy)
 
-        def both(i):
-            @pl.when(has_prev(fx))
-            def _():
-                reduce_step(a, fx, i)
-            reduce_step(a, fy, i)
-        loop(both)
-
-        def gather(i):
-            gather_step(a, fy, i)
-            gather_step(a, fx, i)
-        loop(gather)
+        def slot(t, c):
+            for f in (fy, fx):
+                i = t - (2 * (n_t - 1) - far(f)) * LAG
+
+                @pl.when((i >= 0) & (i < pieces))
+                def _():
+                    gather_step(a, f, i)
+            for f in (fy, fx):
+                i = t - far(f) * LAG
+                ready = (i >= 0) & (i < pieces)
+
+                @pl.when(ready & has_prev(f) if f is fx else ready)
+                def _():
+                    reduce_step(a, f, i)
+            return c
+        lax.fori_loop(0, 2 * (n_t - 1) * LAG + pieces, slot, 0)
 
     @pl.when(has_lo)
     def _():

time: 168 us -> 86.3 us (0.51)
  Pallas kernels: 164 us -> 83.4 us
    pallas_call x1, Pallas kernels: 164 us -> 83.4 us  [shards(): pl.pallas_call(functools.partial(kernel, n_s, n_t, pieces), out_shape=jax...]
where the time goes in v2:
time: 86.3 us; the launch traced here: 86.1 us
  Pallas kernels  83.4 us (97%)
  local copies, waits for them, and re-layouts  2.11 us (2%)
    pallas_call x1, Pallas kernels, shards(): pl.pallas_call(functools.partial(kernel, n_s, n_t, pieces), out_shape=jax...  83.4 us
    unnamed x1, local copies, waits for them, and re-layouts  2.11 us

profile of v2, /device:TPU:4, one launch (start us, length us, event | category | flops | bytes accessed | tf_op | source)
XLA Modules:
  0.0 86.1 jit_solution(8060000494224976832)
XLA Ops:
  0.7 83.4 %shard_map.55 = bf16[640,640]{1,0:T(8,128)(2,1)} custom-call(bf16[640,640]{1,0:T(8,128)(2,1)} %blocks_ref.1, bf16[1,1,640,1920]{3,2,1,0:T(8,128)(2,1)} %left_ref.1, bf16[1,1,640,640]{3,2,1,0:T(8,128)(2,1)} %right_ref.1, s32[1,3]{1,0:T(1,128)} %coup_ref.1, s32[1]{0:T(128)S(6)} %copy.7.width_ref), custom_call_target="tpu_custom_call" | custom-call | tf_op jit(solution)/shard_map/pallas_call | solution.py:274
  84.0 2.1 %copy.8 = bf16[640,640]{1,0:T(8,128)(2,1)} copy(bf16[640,640]{1,0:T(8,128)(2,1)} %shard_map.55) | data formatting | bytes 1638400

commit v3 on v2

--- a/solution.py
+++ b/solution.py
@@ -10,11 +10,12 @@
 MESH = pl.DeviceIdType.MESH
 PIECE = 32
 LAG = 4
-
-
-def kernel(n_s, n_t, pieces, blocks_ref, left_ref, right_ref, coup_ref, width_ref, out_ref,
-           lbuf, rbuf, st1, st2, sbuf, recv, send, obuf,
-           lsem, osem, h1s, h1r, rss, rsr, ags, agr, h2s, h2r):
+SHARED = 0.6
+
+
+def kernel(n_s, n_t, pieces, part, cuts, blocks_ref, left_ref, right_ref, coup_ref, width_ref, out_ref,
+           lbuf, rbuf, st1, st2, tbuf, sbuf, recv, send, obuf,
+           lsem, osem, h1s, h1r, shs, shr, ups, upr, dns, dnr, rss, rsr, ags, agr, h2s, h2r):
     s = lax.axis_index("sector")
     z = lax.axis_index("term")
     side = blocks_ref.shape[0]
@@ -43,21 +44,48 @@
              + has_dn.astype(jnp.int32) + has_up.astype(jnp.int32))
     pl.semaphore_wait(barrier, count)
 
-    def halo1(d):
-        group = 2 if d < 0 else 0
-        slot = 0 if d < 0 else 1
-        return pltpu.make_async_remote_copy(
-            src_ref=blocks_ref, dst_ref=st1.at[pl.ds(group * side, side), :],
-            send_sem=h1s.at[slot], recv_sem=h1r.at[slot],
-            device_id=to_sector(d), device_id_type=MESH)
-
-    @pl.when(has_lo)
-    def _():
-        halo1(-1).start()
-
-    @pl.when(has_hi)
-    def _():
-        halo1(1).start()
+    odd = lax.rem(s, 2)
+    mate = s + 1 - 2 * odd
+    far_s = s - 1 + 2 * odd
+    has_far = (far_s >= 0) & (far_s < n_s)
+    g_mate = 2 - 2 * odd
+    g_far = 2 * odd
+    direct = side - n_t * part
+    cut = part // cuts
+
+    def rows1(group, offset, size):
+        return pl.ds(pl.multiple_of(group * side + offset, 16), size)
+
+    def mate_copy():
+        return pltpu.make_async_remote_copy(
+            src_ref=blocks_ref, dst_ref=st1.at[rows1(2 - g_mate, 0, side), :],
+            send_sem=h1s.at[0], recv_sem=h1r.at[0], device_id=(mate, z), device_id_type=MESH)
+
+    def direct_copy():
+        return pltpu.make_async_remote_copy(
+            src_ref=blocks_ref.at[pl.ds(0, direct), :], dst_ref=st1.at[rows1(2 - g_far, 0, direct), :],
+            send_sem=h1s.at[1], recv_sem=h1r.at[1], device_id=(far_s, z), device_id_type=MESH)
+
+    def part_copy(q):
+        offset = direct + z * part + q * cut
+        return pltpu.make_async_remote_copy(
+            src_ref=blocks_ref.at[pl.ds(pl.multiple_of(offset, 16), cut), :],
+            dst_ref=st1.at[rows1(2 - g_far, offset, cut), :],
+            send_sem=shs.at[q], recv_sem=shr.at[q], device_id=(far_s, z), device_id_type=MESH)
+
+    def pass_copy(owner, q, d):
+        ref = st1.at[rows1(g_far, direct + owner * part + q * cut, cut), :]
+        sends, recvs = (ups, upr) if d > 0 else (dns, dnr)
+        return pltpu.make_async_remote_copy(
+            src_ref=ref, dst_ref=ref, send_sem=sends.at[owner, q], recv_sem=recvs.at[owner, q],
+            device_id=(s, z + d), device_id_type=MESH)
+
+    @pl.when(has_far)
+    def _():
+        for q in range(cuts):
+            part_copy(q).start()
+        direct_copy().start()
+    mate_copy().start()
 
     zeros = jnp.zeros((side, side), st1.dtype)
 
@@ -95,10 +123,17 @@
     def rows_of(f, i):
         return pl.ds(pl.multiple_of(f * half + i * pr, pr), pr)
 
-    def contract(st, f):
+    def cols_of(g):
+        return pl.ds(pl.multiple_of(g * side, 128), side)
+
+    def contract(st, f, a):
         base = pl.ds(pl.multiple_of(f * half, half), half)
-        t = jnp.dot(lbuf[base, :], st[...], preferred_element_type=jnp.float32).astype(jnp.bfloat16)
-        sbuf[base, :] = jnp.dot(t, rbuf[...], preferred_element_type=jnp.float32)
+        if a == 0:
+            t = tbuf[base, :] + jnp.dot(
+                lbuf[base, cols_of(g_far)], st[rows1(g_far, 0, side), :], preferred_element_type=jnp.float32)
+        else:
+            t = jnp.dot(lbuf[base, :], st[...], preferred_element_type=jnp.float32)
+        sbuf[base, :] = jnp.dot(t.astype(jnp.bfloat16), rbuf[...], preferred_element_type=jnp.float32)
 
     def rs_copy(a, f, i):
         r = rows_of(f, i)
@@ -189,13 +224,13 @@
 
     def apply(a, st):
         fx, fy = flows
-        contract(st, fx)
+        contract(st, fx, a)
 
         @pl.when(jnp.logical_not(has_prev(fx)))
         def _():
             loop(lambda i: reduce_step(a, fx, i))
 
-        contract(st, fy)
+        contract(st, fy, a)
 
         def slot(t, c):
             for f in (fy, fx):
@@ -214,13 +249,48 @@
             return c
         lax.fori_loop(0, 2 * (n_t - 1) * LAG + pieces, slot, 0)
 
-    @pl.when(has_lo)
-    def _():
-        halo1(1).wait_recv()
-
-    @pl.when(has_hi)
-    def _():
-        halo1(-1).wait_recv()
+    @pl.when(has_far)
+    def _():
+        for q in range(cuts):
+            part_copy(q).wait_recv()
+
+            @pl.when(has_up)
+            def _():
+                pass_copy(z, q, 1).start()
+
+            @pl.when(has_dn)
+            def _():
+                pass_copy(z, q, -1).start()
+
+    mate_copy().wait_recv()
+    for f in (0, 1):
+        base = pl.ds(f * half, half)
+        tbuf[base, :] = (
+            jnp.dot(lbuf[base, pl.ds(side, side)], st1[pl.ds(side, side), :], preferred_element_type=jnp.float32)
+            + jnp.dot(lbuf[base, cols_of(g_mate)], st1[rows1(g_mate, 0, side), :], preferred_element_type=jnp.float32))
+
+    @pl.when(has_far)
+    def _():
+        def farther(k, c):
+            for q in range(cuts):
+                @pl.when(z - k >= 0)
+                def _():
+                    pass_copy(z - k, q, 1).wait_recv()
+
+                    @pl.when(has_up)
+                    def _():
+                        pass_copy(z - k, q, 1).start()
+
+                @pl.when(z + k < n_t)
+                def _():
+                    pass_copy(z + k, q, -1).wait_recv()
+
+                    @pl.when(has_dn)
+                    def _():
+                        pass_copy(z + k, q, -1).start()
+            return c
+        lax.fori_loop(1, n_t, farther, 0)
+        direct_copy().wait_recv()
     apply(0, st1)
 
     def arrived(i):
@@ -256,23 +326,37 @@
             out_copy(f, i).wait()
     loop(drain)
 
-    @pl.when(has_lo)
-    def _():
-        halo1(-1).wait_send()
-
-    @pl.when(has_hi)
-    def _():
-        halo1(1).wait_send()
+    mate_copy().wait_send()
+
+    @pl.when(has_far)
+    def _():
+        direct_copy().wait_send()
+        for q in range(cuts):
+            part_copy(q).wait_send()
+
+        def passed(owner, c):
+            for q in range(cuts):
+                @pl.when(has_up & (owner <= z))
+                def _():
+                    pass_copy(owner, q, 1).wait_send()
+
+                @pl.when(has_dn & (owner >= z))
+                def _():
+                    pass_copy(owner, q, -1).wait_send()
+            return c
+        lax.fori_loop(0, n_t, passed, 0)
 
 
 def shards(n_s, n_t, blocks, left_env, right_env, coupling, widths):
     side = blocks.shape[1]
     pieces = side // 2 // PIECE
+    part = int(SHARED * side) // (16 * n_t) * 16
+    cuts = max(q for q in (1, 2, 3) if part % (16 * q) == 0)
     dma = pltpu.SemaphoreType.DMA
     any_space = pl.BlockSpec(memory_space=pl.ANY)
     smem = pl.BlockSpec(memory_space=pltpu.SMEM)
     return pl.pallas_call(
-        functools.partial(kernel, n_s, n_t, pieces),
+        functools.partial(kernel, n_s, n_t, pieces, part, cuts),
         out_shape=jax.ShapeDtypeStruct(blocks.shape, blocks.dtype),
         in_specs=[any_space, any_space, any_space, smem, smem],
         out_specs=any_space,
@@ -282,10 +366,13 @@
             pltpu.VMEM((3 * side, side), jnp.bfloat16),
             pltpu.VMEM((3 * side, side), jnp.bfloat16),
             pltpu.VMEM((side, side), jnp.float32),
+            pltpu.VMEM((side, side), jnp.float32),
             pltpu.VMEM((2, side, side), jnp.bfloat16),
             pltpu.VMEM((2, side, side), jnp.bfloat16),
             pltpu.VMEM((side, side), jnp.bfloat16),
             dma((3,)), dma((2, pieces)), dma((2,)), dma((2,)),
+            dma((cuts,)), dma((cuts,)),
+            dma((n_t, cuts)), dma((n_t, cuts)), dma((n_t, cuts)), dma((n_t, cuts)),
             dma((2, 2, pieces)), dma((2, 2, pieces)),
             dma((2, 2, pieces)), dma((2, 2, pieces)),
             dma((2, 2, pieces)), dma((2, 2, pieces)),

time: 86.3 us -> 82.7 us (0.958)
  Pallas kernels: 83.4 us -> 79.8 us
    pallas_call x1, Pallas kernels: 83.4 us -> 79.8 us  [shards(): pl.pallas_call(functools.partial(kernel, n_s, n_t, pieces, part, cuts), o...]
where the time goes in v3:
time: 82.7 us; the launch traced here: 82.5 us
  Pallas kernels  79.8 us (96%)
  local copies, waits for them, and re-layouts  2.11 us (3%)
    pallas_call x1, Pallas kernels, shards(): pl.pallas_call(functools.partial(kernel, n_s, n_t, pieces, part, cuts), o...  79.8 us
    unnamed x1, local copies, waits for them, and re-layouts  2.11 us

profile of v3, /device:TPU:4, one launch (start us, length us, event | category | flops | bytes accessed | tf_op | source)
XLA Modules:
  0.0 82.5 jit_solution(17211470884501855730)
XLA Ops:
  0.7 79.8 %shard_map.55 = bf16[640,640]{1,0:T(8,128)(2,1)} custom-call(bf16[640,640]{1,0:T(8,128)(2,1)} %blocks_ref.1, bf16[1,1,640,1920]{3,2,1,0:T(8,128)(2,1)} %left_ref.1, bf16[1,1,640,640]{3,2,1,0:T(8,128)(2,1)} %right_ref.1, s32[1,3]{1,0:T(1,128)} %coup_ref.1, s32[1]{0:T(128)S(6)} %copy.7.width_ref), custom_call_target="tpu_custom_call" | custom-call | tf_op jit(solution)/shard_map/pallas_call | solution.py:358
  80.4 2.1 %copy.8 = bf16[640,640]{1,0:T(8,128)(2,1)} copy(bf16[640,640]{1,0:T(8,128)(2,1)} %shard_map.55) | data formatting | bytes 1638400

commit v4 on v3

--- a/solution.py
+++ b/solution.py
@@ -10,6 +10,7 @@
 MESH = pl.DeviceIdType.MESH
 PIECE = 32
 LAG = 4
+BLOCKS = 2
 SHARED = 0.6
 
 
@@ -100,13 +101,6 @@
         st2[pl.ds(2 * side, side), :] = zeros
 
     width = width_ref[0]
-    cp_l.wait()
-    for k in range(3):
-        c = coup_ref[0, k].astype(jnp.float32)
-        cols = pl.ds(k * side, side)
-        lbuf[:, cols] = (lbuf[:, cols].astype(jnp.float32) * c).astype(lbuf.dtype)
-    cp_own.wait()
-    cp_r.wait()
 
     x = jnp.where(z * 2 < n_t, 1, 0)
     flows = (x, 1 - x)
@@ -126,8 +120,10 @@
     def cols_of(g):
         return pl.ds(pl.multiple_of(g * side, 128), side)
 
-    def contract(st, f, a):
-        base = pl.ds(pl.multiple_of(f * half, half), half)
+    block = half // BLOCKS
+
+    def contract(st, f, j, a):
+        base = pl.ds(pl.multiple_of(f * half + j * block, block), block)
         if a == 0:
             t = tbuf[base, :] + jnp.dot(
                 lbuf[base, cols_of(g_far)], st[rows1(g_far, 0, side), :], preferred_element_type=jnp.float32)
@@ -224,13 +220,20 @@
 
     def apply(a, st):
         fx, fy = flows
-        contract(st, fx, a)
-
-        @pl.when(jnp.logical_not(has_prev(fx)))
-        def _():
-            loop(lambda i: reduce_step(a, fx, i))
-
-        contract(st, fy, a)
+        def first(j, c):
+            contract(st, fx, j, a)
+
+            @pl.when(jnp.logical_not(has_prev(fx)))
+            def _():
+                for i in range(pieces // BLOCKS):
+                    reduce_step(a, fx, j * (pieces // BLOCKS) + i)
+            return c
+        lax.fori_loop(0, BLOCKS, first, 0)
+
+        def second(j, c):
+            contract(st, fy, j, a)
+            return c
+        lax.fori_loop(0, BLOCKS, second, 0)
 
         def slot(t, c):
             for f in (fy, fx):
@@ -262,34 +265,46 @@
             def _():
                 pass_copy(z, q, -1).start()
 
-    mate_copy().wait_recv()
-    for f in (0, 1):
+    def farther(k, c):
+        for q in range(cuts):
+            @pl.when(has_far & (z - k >= 0))
+            def _():
+                pass_copy(z - k, q, 1).wait_recv()
+
+                @pl.when(has_up)
+                def _():
+                    pass_copy(z - k, q, 1).start()
+
+            @pl.when(has_far & (z + k < n_t))
+            def _():
+                pass_copy(z + k, q, -1).wait_recv()
+
+                @pl.when(has_dn)
+                def _():
+                    pass_copy(z + k, q, -1).start()
+        return c
+
+    def near(f):
         base = pl.ds(f * half, half)
         tbuf[base, :] = (
             jnp.dot(lbuf[base, pl.ds(side, side)], st1[pl.ds(side, side), :], preferred_element_type=jnp.float32)
             + jnp.dot(lbuf[base, cols_of(g_mate)], st1[rows1(g_mate, 0, side), :], preferred_element_type=jnp.float32))
 
+    cp_l.wait()
+    for k in range(3):
+        c = coup_ref[0, k].astype(jnp.float32)
+        cols = pl.ds(k * side, side)
+        lbuf[:, cols] = (lbuf[:, cols].astype(jnp.float32) * c).astype(lbuf.dtype)
+    cp_own.wait()
+    cp_r.wait()
+    mate_copy().wait_recv()
+    farther(1, 0)
+    near(0)
+    lax.fori_loop(2, n_t, farther, 0)
+    near(1)
+
     @pl.when(has_far)
     def _():
-        def farther(k, c):
-            for q in range(cuts):
-                @pl.when(z - k >= 0)
-                def _():
-                    pass_copy(z - k, q, 1).wait_recv()
-
-                    @pl.when(has_up)
-                    def _():
-                        pass_copy(z - k, q, 1).start()
-
-                @pl.when(z + k < n_t)
-                def _():
-                    pass_copy(z + k, q, -1).wait_recv()
-
-                    @pl.when(has_dn)
-                    def _():
-                        pass_copy(z + k, q, -1).start()
-            return c
-        lax.fori_loop(1, n_t, farther, 0)
         direct_copy().wait_recv()
     apply(0, st1)
 

time: 82.7 us -> 81.9 us (level)
  Pallas kernels: 79.8 us -> 78.9 us
    pallas_call x1, Pallas kernels: 79.8 us -> 78.9 us  [shards(): pl.pallas_call(functools.partial(kernel, n_s, n_t, pieces, part, cuts), o...]
where the time goes in v4:
time: 81.9 us; the launch traced here: 81.7 us
  Pallas kernels  78.9 us (96%)
  local copies, waits for them, and re-layouts  2.11 us (3%)
    pallas_call x1, Pallas kernels, shards(): pl.pallas_call(functools.partial(kernel, n_s, n_t, pieces, part, cuts), o...  78.9 us
    unnamed x1, local copies, waits for them, and re-layouts  2.11 us

profile of v4, /device:TPU:4, one launch (start us, length us, event | category | flops | bytes accessed | tf_op | source)
XLA Modules:
  0.0 81.7 jit_solution(10363659623866195067)
XLA Ops:
  0.7 78.9 %shard_map.55 = bf16[640,640]{1,0:T(8,128)(2,1)} custom-call(bf16[640,640]{1,0:T(8,128)(2,1)} %blocks_ref.1, bf16[1,1,640,1920]{3,2,1,0:T(8,128)(2,1)} %left_ref.1, bf16[1,1,640,640]{3,2,1,0:T(8,128)(2,1)} %right_ref.1, s32[1,3]{1,0:T(1,128)} %coup_ref.1, s32[1]{0:T(128)S(6)} %copy.7.width_ref), custom_call_target="tpu_custom_call" | custom-call | tf_op jit(solution)/shard_map/pallas_call | solution.py:373
  79.6 2.1 %copy.8 = bf16[640,640]{1,0:T(8,128)(2,1)} copy(bf16[640,640]{1,0:T(8,128)(2,1)} %shard_map.55) | data formatting | bytes 1638400
